TPU v7x, 256 devices: a whole 4x4x8 slice. The times are simulated.
256 devices in a mesh: slab: 64 (over z, x, core), dom: 4 (over y).
Axes of the slice: x: 4, y: 4, z: 8, core: 2. Of those that a mesh axis runs over, the one named last changes fastest.
Arguments:
- elem_grad: float32 [3, 8, 1376256], P(None, None, ('slab', 'dom')), may hold values from -3 to 3
- elem_stress: float32 [6, 1376256], P(None, ('slab', 'dom')), may hold values from -6 to 6
- elem_grade: int32 [1376256], P(('slab', 'dom')), may hold values from 0 to 15
- grade_scale: float32 [16], replicated, may hold values from 0.5 to 2
- part_counts: int32 [64, 4], P('slab'), may hold values from 1 to 5376, as said below
- node_lists: int32 [4, 128, 8, 512], P(None, 'slab', None, 'dom'), may hold values from -1 to 7167, as said below
- stiff_diag: float32 [3, 128, 8, 512], P(None, 'slab', None, 'dom'), may hold values from 1 to 4
- start_block: float32 [3, 32, 128, 8, 512], P(None, None, 'slab', None, 'dom'), may hold values from -600 to 600
Outputs:
- next_block: float32 [3, 32, 128, 8, 512], P(None, None, 'slab', None, 'dom')
- diag_blocks: float32 [2, 32, 32], replicated
- offdiag_blocks: float32 [3, 32, 32], replicated
Inputs may be any that keep to these rules, and one draw needn't show every extreme that they name: `part_counts`: each row sums to 7168, the elements of one slab; in every slab one partition holds exactly 5376. node_lists[j, f, x, y] is the pool number, within the slab of floor f, of the element of layer f whose in-plane base corner is (x - j mod 2, (y - j // 2) mod 512); it is -1 exactly where x - j mod 2 lies outside 0 to 6. Every element of a slab appears at its four in-plane corners.
All inputs are finite; a program needn't handle non-finite values.
Results may differ from a plain program's by a relative error of at most 0.0003.
Values sent between devices are 32-bit elements; how exact they have to be, the bound alone decides.
No kernel may reach another device: no remote copies, remote signals or barrier semaphores. Data moves between devices by JAX's collectives and lax.ppermute only.
A program may use at most 128 MiB of HBM per device.

v0:
```python
import jax
import jax.numpy as jnp
import numpy as np
from jax import lax
from jax.sharding import PartitionSpec as P

highest = lax.Precision.HIGHEST


def extended_2(cells, sides, width):
    for axis, dim in sides:
        count = lax.axis_size(axis)
        ends = count - 1
        head = lax.slice_in_dim(cells, 0, width, axis=dim)
        tail = lax.slice_in_dim(cells, cells.shape[dim] - width, cells.shape[dim], axis=dim)
        cells = jnp.concatenate(
            [
                lax.ppermute(tail, axis, [(i, (i + 1) % count) for i in range(ends)]),
                cells,
                lax.ppermute(head, axis, [((i + 1) % count, i) for i in range(ends)]),
            ],
            axis=dim,
        )
    return cells


def from_behind(value, axis, steps):
    count = lax.axis_size(axis)
    pairs = [(source, (source + steps) % count) for source in range(count)]
    return lax.ppermute(value, axis, pairs)


def passed_along(block, axis, distance):
    devices = range(lax.axis_size(axis))
    route = [(i - distance, i) for i in devices if i - distance in devices]
    return lax.ppermute(block, axis, route)


def offset_table(quad_slot, layer_side):
    table = np.zeros((8, 27))
    shift_x = quad_slot % 2
    shift_y = quad_slot // 2
    for corner in range(8):
        corner_x = corner % 2
        corner_y = corner // 2 % 2
        corner_z = corner // 4
        target = (
            corner_x - shift_x + 1 + 3 * (corner_y - shift_y + 1) + 9 * (corner_z - layer_side + 1)
        )
        table[corner, target] = 1.0
    return jnp.asarray(table, dtype=jnp.float32)


def stress_matrix(stress):
    return jnp.stack(
        [
            jnp.stack([stress[0], stress[5], stress[4]]),
            jnp.stack([stress[5], stress[1], stress[3]]),
            jnp.stack([stress[4], stress[3], stress[2]]),
        ]
    )


def grade_lookup(grades, table):
    levels = jnp.arange(table.shape[0], dtype=jnp.int32)[:, None]
    onehot = (grades[None, :] == levels).astype(jnp.float32)
    return jnp.dot(table, onehot, precision=highest)


def element_matrices(gradients, stress, scales):
    pushed = jnp.einsum("ik...,kb...->ib...", stress_matrix(stress), gradients, precision=highest)
    return jnp.einsum("ia...,ib...->ab...", gradients, pushed, precision=highest) * scales


def pool_columns(slot_lists, counts, capacity):
    offsets = jnp.cumsum(counts) - counts
    shaped = offsets.reshape((-1,) + (1,) * slot_lists.ndim)
    pool_ids = jnp.maximum(slot_lists, 0)
    partition = jnp.sum((pool_ids[None] >= shaped[1:]).astype(jnp.int32), axis=0)
    levels = jnp.arange(counts.shape[0], dtype=jnp.int32).reshape(shaped.shape)
    starts = jnp.sum(jnp.where(partition[None] == levels, shaped, 0), axis=0)
    columns = partition * capacity + pool_ids - starts
    return (columns, (slot_lists >= 0).astype(jnp.float32))


def accumulate(getter, present):
    sides = []
    for layer_side in range(2):
        summed = None
        for quad_slot in range(4):
            row_values = getter(quad_slot, layer_side) * present[quad_slot]
            contribution = jnp.einsum(
                "bfxy,bo->ofxy", row_values, offset_table(quad_slot, layer_side), precision=highest
            )
            summed = contribution if summed is None else summed + contribution
        sides.append(summed)
    return (sides[0], sides[1])


def apply_operator(block, stencil, diagonal):
    extended = extended_2(block, (("slab", 2),), 1)
    edge_shape = extended.shape[:4]
    first_column = extended[..., 0].reshape(-1)
    last_column = extended[..., -1].reshape(-1)
    from_left = from_behind(last_column, "dom", 1).reshape(edge_shape + (1,))
    from_right = from_behind(first_column, "dom", -1).reshape(edge_shape + (1,))
    extended = jnp.concatenate([from_left, extended, from_right], axis=4)
    padded = jnp.pad(extended, ((0, 0), (0, 0), (0, 0), (1, 1), (0, 0)))
    floors, across, beside_all = (block.shape[2], block.shape[3], block.shape[4])
    result = diagonal[:, None] * block
    for offset in range(27):
        step_x = offset % 3
        step_y = offset // 3 % 3
        step_z = offset // 9
        result = (
            result
            + stencil[offset]
            * padded[
                :,
                :,
                step_z : step_z + floors,
                step_x : step_x + across,
                step_y : step_y + beside_all,
            ]
        )
    return result


def local_inner(first_block, second_block):
    return jnp.einsum("cvfxy,cwfxy->vw", first_block, second_block, precision=highest)


def mix(block, matrix):
    return jnp.einsum("cvfxy,vw->cwfxy", block, matrix, precision=highest)


def normalize(block, gram_matrix):
    factor = jnp.linalg.cholesky(gram_matrix)
    identity = jnp.eye(gram_matrix.shape[0], dtype=jnp.float32)
    inverse = lax.linalg.triangular_solve(factor, identity, left_side=True, lower=True)
    return (jnp.einsum("cvfxy,wv->cwfxy", block, inverse, precision=highest), factor.T)


def advance(basis_block, image_block, dof_count):
    projection = lax.psum(local_inner(basis_block, image_block), ("slab", "dom")) / dof_count
    residual = image_block - mix(basis_block, projection)
    gram_matrix = lax.psum(local_inner(residual, residual), ("slab", "dom")) / dof_count
    following, upper_factor = normalize(residual, gram_matrix)
    return (following, projection, upper_factor)


def per_device(
    elem_grad,
    elem_stress,
    elem_grade,
    grade_scale,
    part_counts,
    node_lists,
    stiff_diag,
    start_block,
):
    capacity = elem_grad.shape[2]
    counts = part_counts[0]
    columns, present = pool_columns(node_lists, counts, capacity)
    flat_columns = columns.reshape(-1)
    slot_shape = node_lists.shape
    scales = grade_lookup(elem_grade, grade_scale)
    matrices = element_matrices(elem_grad, elem_stress, scales).reshape(64, capacity)
    shard_piece = lax.all_gather(matrices, "dom", axis=1, tiled=True)
    inside = (flat_columns >= 0) & (flat_columns < shard_piece.shape[1])
    selected = jnp.take(shard_piece, jnp.clip(flat_columns, 0, shard_piece.shape[1] - 1), axis=1)
    picked = jnp.where(inside[None, :], selected, 0.0)
    picked = picked.reshape((8, 8) + slot_shape)

    def getter(quad_slot, layer_side):
        return picked[quad_slot + 4 * layer_side, :, quad_slot]

    bottom, top_side = accumulate(getter, present)
    below = passed_along(bottom[:, 0], "slab", -1)
    stencil = top_side + jnp.concatenate([bottom[:, 1:], below[:, None]], axis=1)
    dof_count = (
        3
        * start_block.shape[2]
        * start_block.shape[3]
        * start_block.shape[4]
        * lax.axis_size("slab")
        * lax.axis_size("dom")
    )
    start_gram = lax.psum(local_inner(start_block, start_block), ("slab", "dom")) / dof_count
    first, start_factor = normalize(start_block, start_gram)
    image_block = apply_operator(first, stencil, stiff_diag)
    second, alpha_one, beta_one = advance(first, image_block, dof_count)
    image_block = apply_operator(second, stencil, stiff_diag) - mix(first, beta_one.T)
    third, alpha_two, beta_two = advance(second, image_block, dof_count)
    return (third, jnp.stack([alpha_one, alpha_two]), jnp.stack([start_factor, beta_one, beta_two]))


def solution(mesh):
    in_specs = (
        P(None, None, ("slab", "dom")),
        P(None, ("slab", "dom")),
        P(("slab", "dom")),
        P(),
        P("slab", None),
        P(None, "slab", None, "dom"),
        P(None, "slab", None, "dom"),
        P(None, None, "slab", None, "dom"),
    )
    out_specs = (P(None, None, "slab", None, "dom"), P(), P())
    return jax.shard_map(
        per_device, mesh=mesh, in_specs=in_specs, out_specs=out_specs, check_vma=False
    )
```

profile of v0, /device:TPU:1, one launch (start us, length us, event | category | flops | bytes accessed | tf_op | source)
XLA Modules:
  0.0 704.9 jit_solution(14707492040384633531)
XLA Ops:
  9.1 7.5 %copy.136 = f32[3,3,5376]{1,0,2:T(4,128)} copy(f32[3,3,5376]{2,1,0:T(4,128)S(1)} %pad_maximum_fusion.18) | data formatting | bytes 387072 | tf_op jit(solution)/shard_map/stack | solution.py:55
  16.6 7.2 %copy.137 = f32[3,8,5376]{1,0,2:T(4,128)} copy(f32[3,8,5376]{2,1,0:T(8,128)S(1)} %copy-done.12) | data formatting | bytes 1032192 | tf_op args[0]
  23.9 39.3 %fusion.144 = f32[5376,3,8]{2,1,0:T(4,128)S(1)} fusion(f32[3,3,5376]{1,0,2:T(4,128)} %copy.136, f32[3,8,5376]{1,0,2:T(4,128)} %copy.137), kind=kOutput, calls=%fused_computation.282 | convolution fusion | flops 4644864 | bytes 1225728 | tf_op jit(solution)/shard_map/ik...,kb...->ib.../dot_general | solution.py:71
  63.5 57.4 %multiply_bitcast_fusion = f32[8,8,5376]{0,1,2:T(8,128)} fusion(f32[5376]{0:T(1024)S(1)} %convolution_reduce_fusion, f32[3,8,5376]{1,0,2:T(4,128)S(1)} %copy-done.2, f32[5376,3,8]{2,1,0:T(4,128)S(1)} %fusion.144), kind=kOutput, calls=%fused_computation.1 | convolution fusion | flops 12730368 | bytes 2429952 | tf_op jit(solution)/shard_map/ia...,ib...->ab.../dot_general | solution.py:72
  120.9 12.2 %copy.139 = f32[8,8,5376]{2,1,0:T(8,128)S(1)} copy(f32[8,8,5376]{0,1,2:T(8,128)} %multiply_bitcast_fusion) | data formatting | bytes 2752512 | tf_op jit(solution)/shard_map/mul | solution.py:72
  133.1 2.1 copy.140
  136.2 82.3 %psum.35 = f32[32,32]{0,1:T(8,128)S(1)} all-reduce(f32[32,32]{0,1:T(8,128)S(1)} %convolution_bitcast_fusion.10), channel_id=1, replica_groups=mesh['slab'=64,'dom'=4] {'slab','dom'}, use_global_device_ids=true, to_apply=%region_0.0 | all-reduce | flops 1024 | bytes 8192 | tf_op jit(solution)/shard_map/psum | solution.py:189
  218.5 2.9 cholesky.59
  223.4 2.4 custom-call.7
  227.1 2.2 collective-permute-start.1
  229.2 2.4 collective-permute-start.2
  233.9 4.8 collective-permute-done.2
  238.9 1.7 fusion.137
  240.6 3.8 copy.154
  244.9 2.4 copy.155
  247.5 2.5 collective-permute-start.4
  250.8 2.3 copy.156
  253.4 3.5 copy.157
  256.9 4.5 select_maximum_fusion.4
  261.4 31.8 %gather_fusion = f32[8192,64]{1,0:T(8,128)} fusion(f32[64,21504]{0,1:T(8,128)} %all-gather.2.cloned.1.call-done, s32[8192]{0:T(1024)S(1)} %copy-done.13), kind=kCustom, calls=%fused_computation | custom fusion | bytes 4227072 | tf_op jit(solution)/shard_map/jit(_take)/gather | solution.py:171
  293.2 3.8 copy.141
  297.1 2.0 copy.205
  301.3 2.3 collective-permute-start
  304.9 2.7 collective-permute-done
  308.5 5.3 fusion.41
  314.9 81.3 %psum.36 = f32[32,32]{0,1:T(8,128)S(1)} all-reduce(f32[32,32]{0,1:T(8,128)S(1)} %convolution_bitcast_fusion.9), channel_id=1, replica_groups=mesh['slab'=64,'dom'=4] {'slab','dom'}, use_global_device_ids=true, to_apply=%region_6.9 | all-reduce | flops 1024 | bytes 8192 | tf_op jit(solution)/shard_map/psum | solution.py:145
  397.7 73.5 %psum.37 = f32[32,32]{0,1:T(8,128)S(1)} all-reduce(f32[32,32]{0,1:T(8,128)S(1)} %convolution_bitcast_fusion.8), channel_id=1, replica_groups=mesh['slab'=64,'dom'=4] {'slab','dom'}, use_global_device_ids=true, to_apply=%region_7.10 | all-reduce | flops 1024 | bytes 8192 | tf_op jit(solution)/shard_map/psum | solution.py:147
  471.3 2.9 cholesky.70
  476.2 2.4 custom-call.8
  479.8 3.5 collective-permute-start.5
  483.3 1.9 collective-permute-start.6
  485.2 2.8 collective-permute-done.5
  488.0 4.4 collective-permute-done.6
  493.2 1.7 fusion.136
  495.0 4.4 copy.163
  499.4 1.7 reshape_squeeze.14
  501.3 3.0 copy.164
  504.3 1.7 reshape_squeeze.15
  506.0 2.7 collective-permute-start.8
  510.9 3.2 copy.165
  515.8 4.4 copy.166
  520.4 3.4 select_maximum_fusion
  524.1 7.2 %fusion.10 = f32[3,32,2,8,128]{4,1,3,2,0:T(8,128)S(1)} fusion(f32[3,32,4,10,130]{4,1,3,2,0:T(8,128)S(1)} %select_maximum_fusion, f32[3,32,4,8,1]{4,1,3,2,0:T(8,128)S(1)} %copy-done.5, f32[3,32,1,8,128]{4,1,3,2,0:T(8,128)S(1)} %copy-done.11, f32[3,32,2,8,128]{4,1,3,2,0:T(8,128)S(1)} %convolution_bitcast_fusion.3, ...), kind=kOutput, calls=%fused_computation.45 | convolution fusion | flops 90442752 | bytes 17575936 | tf_op jit(solution)/shard_map/cvfxy,vw->cwfxy/dot_general | solution.py:134
  533.0 78.2 %psum.38 = f32[32,32]{0,1:T(8,128)S(1)} all-reduce(f32[32,32]{0,1:T(8,128)S(1)} %convolution_bitcast_fusion.7), channel_id=1, replica_groups=mesh['slab'=64,'dom'=4] {'slab','dom'}, use_global_device_ids=true, to_apply=%region_8.11 | all-reduce | flops 1024 | bytes 8192 | tf_op jit(solution)/shard_map/psum | solution.py:145
  611.2 1.9 fusion.5
  613.9 73.4 %psum.39 = f32[32,32]{0,1:T(8,128)S(1)} all-reduce(f32[32,32]{0,1:T(8,128)S(1)} %convolution_bitcast_fusion.6), channel_id=1, replica_groups=mesh['slab'=64,'dom'=4] {'slab','dom'}, use_global_device_ids=true, to_apply=%region_9.12 | all-reduce | flops 1024 | bytes 8192 | tf_op jit(solution)/shard_map/psum | solution.py:147
  687.4 2.9 cholesky.81
  693.0 2.4 custom-call.9
  (268 shorter events, 32.7 us)
Async XLA Ops:
  7.2 56.1 %copy-start = (f32[16]{0:T(128)S(1)}, f32[16]{0:T(128)}, u32[]{:S(2)}) copy-start(f32[16]{0:T(128)} %param.22) | copy-start | bytes 196
  7.2 254.2 %all-gather.2.cloned.1.call-start = ((), (), s32[]{:S(2)}) async-start(), calls=%async_computation | async-start | bytes 13762560 | tf_op jit(solution)/shard_map/all_gather | solution.py:169
  9.1 7.5 %copy-start.12 = (f32[3,8,5376]{2,1,0:T(8,128)S(1)}, f32[3,8,5376]{2,1,0:T(8,128)}, u32[]{:S(2)}) copy-start(f32[3,8,5376]{2,1,0:T(8,128)} %param.19) | copy-start | bytes 1548292
  23.9 39.4 %copy-start.89 = (s32[5376]{0:T(1024)S(1)}, s32[5376]{0:T(1024)}, u32[]{:S(2)}) copy-start(s32[5376]{0:T(1024)} %param.21) | copy-start | bytes 64516
  23.9 39.6 %copy-start.2 = (f32[3,8,5376]{1,0,2:T(4,128)S(1)}, f32[3,8,5376]{1,0,2:T(4,128)}, u32[]{:S(2)}) copy-start(f32[3,8,5376]{1,0,2:T(4,128)} %copy.137) | copy-start | bytes 1548292
  135.2 96.4 %copy-start.90 = (s32[1,4]{1,0:T(1,128)S(1)}, s32[1,4]{1,0:T(1,128)}, u32[]{:S(2)}) copy-start(s32[1,4]{1,0:T(1,128)} %param.23) | copy-start | bytes 52
  135.2 96.7 %copy-start.14 = (s32[4,2,8,128]{3,2,1,0:T(8,128)S(1)}, s32[4,2,8,128]{3,2,1,0:T(8,128)}, u32[]{:S(2)}) copy-start(s32[4,2,8,128]{3,2,1,0:T(8,128)} %param.24) | copy-start | bytes 98308
  227.1 6.9 collective-permute-start.1
  229.2 9.5 %collective-permute-start.2 = (f32[3,32,1,8,128]{4,1,3,2,0:T(8,128)S(1)}, f32[3,32,1,8,128]{4,1,3,2,0:T(8,128)S(1)}, u32[]{:S(2)}, u32[]{:S(2)}) collective-permute-start(f32[3,32,1,8,128]{4,1,3,2,0:T(8,128)S(1)} %get-tuple-element.40), channel_id=1, source_target_pairs={{4,0},{8,4},{12,8},{16,12},{20,16},{24,20},{28,24},{32,28},{36,32}... | collective-permute-start | bytes 1179656 | tf_op jit(solution)/shard_map/ppermute | solution.py:20
  238.7 18.1 %copy-start.6 = (f32[3,32,1,8,128]{4,1,3,2,0:T(8,128)}, f32[3,32,1,8,128]{4,1,3,2,0:T(8,128)S(1)}, u32[]{:S(2)}) copy-start(f32[3,32,1,8,128]{4,1,3,2,0:T(8,128)S(1)} %collective-permute-done.2) | copy-start | bytes 1179652
  238.8 11.1 %copy-start.15 = (f32[4,2,8,128]{3,2,1,0:T(8,128)S(1)}, f32[4,2,8,128]{3,2,1,0:T(8,128)}, u32[]{:S(2)}) copy-start(f32[4,2,8,128]{3,2,1,0:T(8,128)} %get-tuple-element.80) | copy-start | bytes 98308
  244.5 6.0 collective-permute-start.3
  247.5 5.7 collective-permute-start.4
  293.2 5.9 copy-start.78
  299.2 8.4 %copy-start.81 = (f32[8,27,1,1]{1,0,3,2:T(8,128)S(1)}, f32[8,27,1,1]{1,0,3,2:T(8,128)}, u32[]{:S(2)}) copy-start(f32[8,27,1,1]{1,0,3,2:T(8,128)} %constant.100) | copy-start | bytes 2596
  299.4 9.0 %copy-start.3 = (f32[3,32,4,10,130]{4,1,3,2,0:T(8,128)S(1)}, f32[3,32,4,10,130]{4,1,3,2,0:T(8,128)}, u32[]{:S(2)}) copy-start(f32[3,32,4,10,130]{4,1,3,2,0:T(8,128)} %select_maximum_fusion.4) | copy-start | bytes 5990404
  299.4 9.0 %copy-start.4 = (f32[3,32,4,8,1]{4,1,3,2,0:T(8,128)S(1)}, f32[3,32,4,8,1]{4,1,3,2,0:T(8,128)}, u32[]{:S(2)}) copy-start(f32[3,32,4,8,1]{4,1,3,2,0:T(8,128)} %copy.157) | copy-start | bytes 36868
  299.5 9.0 %copy-start.7 = (f32[3,32,1,8,128]{4,1,3,2,0:T(8,128)S(1)}, f32[3,32,1,8,128]{4,1,3,2,0:T(8,128)}, u32[]{:S(2)}) copy-start(f32[3,32,1,8,128]{4,1,3,2,0:T(8,128)} %copy-done.6) | copy-start | bytes 1179652
  299.5 9.0 %copy-start.79 = (f32[3,2,8,128]{3,2,1,0:T(8,128)S(1)}, f32[3,2,8,128]{3,2,1,0:T(8,128)}, u32[]{:S(2)}) copy-start(f32[3,2,8,128]{3,2,1,0:T(8,128)} %param.25) | copy-start | bytes 73732
  301.3 6.3 collective-permute-start
  308.1 5.7 copy-start.21
  308.1 5.7 copy-start.23
  308.1 5.7 copy-start.25
  308.1 5.7 copy-start.27
  308.1 5.7 copy-start.29
  308.1 5.7 copy-start.31
  308.1 5.7 copy-start.33
  308.2 5.7 copy-start.35
  308.2 5.7 copy-start.37
  308.2 5.7 copy-start.39
  308.2 5.7 copy-start.41
  308.2 5.7 copy-start.43
  308.2 5.7 copy-start.45
  308.2 5.7 copy-start.47
  308.2 5.7 copy-start.49
  308.2 5.7 copy-start.51
  308.2 5.7 copy-start.53
  308.3 5.7 copy-start.55
  308.3 5.7 copy-start.57
  308.3 5.7 copy-start.59
  479.8 8.2 %collective-permute-start.5 = (f32[3,32,1,8,128]{4,1,3,2,0:T(8,128)S(1)}, f32[3,32,1,8,128]{4,1,3,2,0:T(8,128)S(1)}, u32[]{:S(2)}, u32[]{:S(2)}) collective-permute-start(f32[3,32,1,8,128]{4,1,3,2,0:T(8,128)S(1)} %get-tuple-element.37), channel_id=1, source_target_pairs={{0,4},{4,8},{8,12},{12,16},{16,20},{20,24},{24,28},{28,32},{32,36}... | collective-permute-start | bytes 1179656 | tf_op jit(solution)/shard_map/ppermute | solution.py:18
  483.3 9.1 %collective-permute-start.6 = (f32[3,32,1,8,128]{4,1,3,2,0:T(8,128)S(1)}, f32[3,32,1,8,128]{4,1,3,2,0:T(8,128)S(1)}, u32[]{:S(2)}, u32[]{:S(2)}) collective-permute-start(f32[3,32,1,8,128]{4,1,3,2,0:T(8,128)S(1)} %get-tuple-element.38), channel_id=1, source_target_pairs={{4,0},{8,4},{12,8},{16,12},{20,16},{24,20},{28,24},{32,28},{36,32}... | collective-permute-start | bytes 1179656 | tf_op jit(solution)/shard_map/ppermute | solution.py:20
  501.1 8.2 %collective-permute-start.7 = (f32[3072]{0:T(1024)}, f32[3072]{0:T(1024)}, u32[]{:S(2)}, u32[]{:S(2)}) collective-permute-start(f32[3072]{0:T(1024)} %reshape_squeeze.14), channel_id=1, source_target_pairs={{0,1},{1,2},{2,3},{3,0},{4,5},{5,6},{6,7},{7,4},{8,9},{9,10},{10,1... | collective-permute-start | bytes 36872 | tf_op jit(solution)/shard_map/ppermute | solution.py:30
  506.0 8.1 %collective-permute-start.8 = (f32[3072]{0:T(1024)}, f32[3072]{0:T(1024)}, u32[]{:S(2)}, u32[]{:S(2)}) collective-permute-start(f32[3072]{0:T(1024)} %reshape_squeeze.15), channel_id=1, source_target_pairs={{0,3},{1,0},{2,1},{3,2},{4,7},{5,4},{6,5},{7,6},{8,11},{9,8},{10,9... | collective-permute-start | bytes 36872 | tf_op jit(solution)/shard_map/ppermute | solution.py:30
  532.2 159.4 %copy-start.18 = (f32[1,32,32]{1,2,0:T(8,128)S(1)}, f32[1,32,32]{1,2,0:T(8,128)}, u32[]{:S(2)}) copy-start(f32[1,32,32]{1,2,0:T(8,128)} %get-tuple-element.84) | copy-start | bytes 12292
  532.2 159.4 %copy-start.19 = (f32[1,32,32]{1,2,0:T(8,128)S(1)}, f32[1,32,32]{1,2,0:T(8,128)}, u32[]{:S(2)}) copy-start(f32[1,32,32]{1,2,0:T(8,128)} %get-tuple-element.86) | copy-start | bytes 12292
  532.2 160.2 %copy-start.20 = (f32[1,32,32]{1,2,0:T(8,128)S(1)}, f32[1,32,32]{1,2,0:T(8,128)}, u32[]{:S(2)}) copy-start(f32[1,32,32]{1,2,0:T(8,128)} %multiply_bitcast_fusion.2) | copy-start | bytes 12292
  532.2 165.7 %copy-start.1 = (f32[16]{0:T(128)S(1)}, f32[16]{0:T(128)}, u32[]{:S(2)}) copy-start(f32[16]{0:T(128)} %param.22) | copy-start | bytes 196
  (53 other events, 197.1 us)
Sparse Core Ops, SparseCore 0:
  135.3 112.6 all-gather.1
where the time goes:
time: 713 us; the launch traced here: 705 us
  blocking collectives  389 us (55%)
  matrix products  117 us (16%)
  local copies, waits for them, and re-layouts  112 us (16%)
  other arithmetic  37.7 us (5%)
  starting transfers between devices  18 us (3%)
  between operations  15.9 us (2%)
  waiting for transfers between devices  15.2 us (2%)
    psum x2, blocking collectives, advance(): lax.psum(local_inner(basis_block, image_block), ('slab', 'dom')) / dof_count  160 us
    psum x2, blocking collectives, advance(): lax.psum(local_inner(residual, residual), ('slab', 'dom')) / dof_count  147 us
    psum x1, blocking collectives, per_device(): lax.psum(local_inner(start_block, start_block), ('slab', 'dom')) / dof_count  82.3 us
    dot_general x1, matrix products, element_matrices(): jnp.einsum('ia...,ib...->ab...', gradients, pushed, precision=highest)  57.4 us
    dot_general x1, matrix products, element_matrices(): jnp.einsum('ik...,kb...->ib...', stress_matrix(stress), gradients, precis...  39.3 us
    gather x2, local copies, waits for them, and re-layouts, per_device(): jnp.take(shard_piece, jnp.clip(flat_columns, 0, shard_piece.shape[1] - 1)...  35.7 us
  transfers between devices with their start and end apart: 10, of which 5 were waited for; matrix products, arithmetic and copies ran while one was open for 6% of the time, Pallas kernels for 0%

commit v1 on v0

--- a/solution.py
+++ b/solution.py
@@ -144,7 +144,7 @@
 def advance(basis_block, image_block, dof_count):
     projection = lax.psum(local_inner(basis_block, image_block), ("slab", "dom")) / dof_count
     residual = image_block - mix(basis_block, projection)
-    gram_matrix = lax.psum(local_inner(residual, residual), ("slab", "dom")) / dof_count
+    gram_matrix = lax.psum(lax.psum(local_inner(residual, residual), "dom"), "slab") / dof_count
     following, upper_factor = normalize(residual, gram_matrix)
     return (following, projection, upper_factor)
 

time: 713 us -> 1090 us (1.53)
  blocking collectives: 389 us -> 762 us
    psum x2 -> x4, blocking collectives: 147 us -> 516 us  [the longest x2 490 us: advance(): lax.psum(lax.psum(local_inner(residual, residual), 'dom'), 'slab')]
  transfers between devices with their start and end apart: 10 -> 10, of which waited for: 5 -> 4; matrix products, arithmetic and copies ran while one was open for 6% -> 4% of each run, Pallas kernels for 0% -> 0%
where the time goes in v1:
time: 1090 us; the launch traced here: 1080 us
  blocking collectives  762 us (70%)
  matrix products  117 us (11%)
  local copies, waits for them, and re-layouts  112 us (10%)
  other arithmetic  37.6 us (3%)
  starting transfers between devices  21.5 us (2%)
  between operations  15.9 us (1%)
  waiting for transfers between devices  11.8 us (1%)
    psum x2, blocking collectives, advance(): lax.psum(lax.psum(local_inner(residual, residual), 'dom'), 'slab')  490 us
    psum x2, blocking collectives, advance(): lax.psum(local_inner(basis_block, image_block), ('slab', 'dom')) / dof_count  164 us
    psum x1, blocking collectives, per_device(): lax.psum(local_inner(start_block, start_block), ('slab', 'dom')) / dof_count  82.3 us
    dot_general x1, matrix products, element_matrices(): jnp.einsum('ia...,ib...->ab...', gradients, pushed, precision=highest)  57.4 us
    dot_general x1, matrix products, element_matrices(): jnp.einsum('ik...,kb...->ib...', stress_matrix(stress), gradients, precis...  39.3 us
    gather x2, local copies, waits for them, and re-layouts, per_device(): jnp.take(shard_piece, jnp.clip(flat_columns, 0, shard_piece.shape[1] - 1)...  35.6 us
    psum x2, blocking collectives, advance(): lax.psum(local_inner(residual, residual), 'dom')  26 us
  transfers between devices with their start and end apart: 10, of which 4 were waited for; matrix products, arithmetic and copies ran while one was open for 4% of the time, Pallas kernels for 0%

profile of v1, /device:TPU:1, one launch (start us, length us, event | category | flops | bytes accessed | tf_op | source)
XLA Modules:
  0.0 1077.9 jit_solution(9051619496053149823)
XLA Ops:
  9.1 7.4 copy.136
  16.6 7.3 copy.137
  23.9 39.3 %fusion.144 = f32[5376,3,8]{2,1,0:T(4,128)S(1)} fusion(f32[3,3,5376]{1,0,2:T(4,128)} %copy.136, f32[3,8,5376]{1,0,2:T(4,128)} %copy.137), kind=kOutput, calls=%fused_computation.282 | convolution fusion | flops 4644864 | bytes 1225728 | tf_op jit(solution)/shard_map/ik...,kb...->ib.../dot_general | solution.py:71
  63.5 57.4 %multiply_bitcast_fusion = f32[8,8,5376]{0,1,2:T(8,128)} fusion(f32[5376]{0:T(1024)S(1)} %convolution_reduce_fusion, f32[3,8,5376]{1,0,2:T(4,128)S(1)} %copy-done.2, f32[5376,3,8]{2,1,0:T(4,128)S(1)} %fusion.144), kind=kOutput, calls=%fused_computation.1 | convolution fusion | flops 12730368 | bytes 2429952 | tf_op jit(solution)/shard_map/ia...,ib...->ab.../dot_general | solution.py:72
  120.8 12.2 %copy.139 = f32[8,8,5376]{2,1,0:T(8,128)S(1)} copy(f32[8,8,5376]{0,1,2:T(8,128)} %multiply_bitcast_fusion) | data formatting | bytes 2752512 | tf_op jit(solution)/shard_map/mul | solution.py:72
  133.0 2.1 copy.140
  136.1 82.3 %psum.49 = f32[32,32]{0,1:T(8,128)S(1)} all-reduce(f32[32,32]{0,1:T(8,128)S(1)} %convolution_bitcast_fusion.10), channel_id=1, replica_groups=mesh['slab'=64,'dom'=4] {'slab','dom'}, use_global_device_ids=true, to_apply=%region_0.0 | all-reduce | flops 1024 | bytes 8192 | tf_op jit(solution)/shard_map/psum | solution.py:189
  218.5 2.9 cholesky.59
  223.3 2.4 custom-call.7
  227.0 2.2 collective-permute-start.1
  229.2 2.4 collective-permute-start.2
  233.9 4.8 collective-permute-done.2
  238.8 1.7 fusion.137
  240.5 3.8 copy.154
  244.8 2.4 copy.155
  247.4 2.5 collective-permute-start.4
  250.7 2.3 copy.156
  253.3 3.5 copy.157
  256.8 4.5 select_maximum_fusion.4
  261.3 31.8 %gather_fusion = f32[8192,64]{1,0:T(8,128)} fusion(f32[64,21504]{0,1:T(8,128)} %all-gather.2.cloned.1.call-done, s32[8192]{0:T(1024)S(1)} %copy-done.13), kind=kCustom, calls=%fused_computation | custom fusion | bytes 4227072 | tf_op jit(solution)/shard_map/jit(_take)/gather | solution.py:171
  293.2 3.8 copy.141
  297.0 2.0 copy.205
  301.2 2.4 collective-permute-start
  304.8 2.6 collective-permute-done
  308.4 5.3 fusion.41
  314.8 81.3 %psum.50 = f32[32,32]{0,1:T(8,128)S(1)} all-reduce(f32[32,32]{0,1:T(8,128)S(1)} %convolution_bitcast_fusion.9), channel_id=1, replica_groups=mesh['slab'=64,'dom'=4] {'slab','dom'}, use_global_device_ids=true, to_apply=%region_6.9 | all-reduce | flops 1024 | bytes 8192 | tf_op jit(solution)/shard_map/psum | solution.py:145
  397.6 12.9 %psum.51 = f32[32,32]{0,1:T(8,128)S(1)} all-reduce(f32[32,32]{0,1:T(8,128)S(1)} %convolution_bitcast_fusion.8), channel_id=1, replica_groups=mesh['slab'=64,'dom'=4] {'dom'}, use_global_device_ids=true, to_apply=%region_7.10 | all-reduce | flops 1024 | bytes 8192 | tf_op jit(solution)/shard_map/psum | solution.py:147
  410.5 244.9 %psum.52 = f32[32,32]{0,1:T(8,128)S(1)} all-reduce(f32[32,32]{0,1:T(8,128)S(1)} %psum.51), channel_id=1, replica_groups=mesh['slab'=64,'dom'=4] {'slab'}, use_global_device_ids=true, to_apply=%region_8.11 | all-reduce | flops 1024 | bytes 8192 | tf_op jit(solution)/shard_map/psum | solution.py:147
  655.5 2.9 cholesky.70
  660.4 2.4 custom-call.8
  663.9 3.6 collective-permute-start.5
  667.6 5.3 collective-permute-start.6
  672.8 3.8 collective-permute-done.6
  677.5 1.7 fusion.136
  679.2 4.4 copy.163
  685.5 3.0 copy.164
  688.5 1.7 reshape_squeeze.15
  690.3 2.7 collective-permute-start.8
  695.2 3.2 copy.165
  700.0 4.4 copy.166
  704.7 3.4 select_maximum_fusion
  708.4 7.1 fusion.10
  717.2 82.3 %psum.53 = f32[32,32]{0,1:T(8,128)S(1)} all-reduce(f32[32,32]{0,1:T(8,128)S(1)} %convolution_bitcast_fusion.7), channel_id=1, replica_groups=mesh['slab'=64,'dom'=4] {'slab','dom'}, use_global_device_ids=true, to_apply=%region_9.12 | all-reduce | flops 1024 | bytes 8192 | tf_op jit(solution)/shard_map/psum | solution.py:145
  799.5 1.9 fusion.5
  802.2 13.1 %psum.54 = f32[32,32]{0,1:T(8,128)S(1)} all-reduce(f32[32,32]{0,1:T(8,128)S(1)} %convolution_bitcast_fusion.6), channel_id=1, replica_groups=mesh['slab'=64,'dom'=4] {'dom'}, use_global_device_ids=true, to_apply=%region_10.13 | all-reduce | flops 1024 | bytes 8192 | tf_op jit(solution)/shard_map/psum | solution.py:147
  815.4 244.9 %psum.55 = f32[32,32]{0,1:T(8,128)S(1)} all-reduce(f32[32,32]{0,1:T(8,128)S(1)} %psum.54), channel_id=1, replica_groups=mesh['slab'=64,'dom'=4] {'slab'}, use_global_device_ids=true, to_apply=%region_11.14 | all-reduce | flops 1024 | bytes 8192 | tf_op jit(solution)/shard_map/psum | solution.py:147
  1060.4 2.9 cholesky.81
  1066.1 2.4 custom-call.9
  (270 shorter events, 34.3 us)
Async XLA Ops:
  7.2 56.0 %copy-start = (f32[16]{0:T(128)S(1)}, f32[16]{0:T(128)}, u32[]{:S(2)}) copy-start(f32[16]{0:T(128)} %param.22) | copy-start | bytes 196
  7.2 254.1 %all-gather.2.cloned.1.call-start = ((), (), s32[]{:S(2)}) async-start(), calls=%async_computation | async-start | bytes 13762560 | tf_op jit(solution)/shard_map/all_gather | solution.py:169
  9.1 7.5 copy-start.12
  23.9 39.3 %copy-start.89 = (s32[5376]{0:T(1024)S(1)}, s32[5376]{0:T(1024)}, u32[]{:S(2)}) copy-start(s32[5376]{0:T(1024)} %param.21) | copy-start | bytes 64516
  23.9 39.6 %copy-start.2 = (f32[3,8,5376]{1,0,2:T(4,128)S(1)}, f32[3,8,5376]{1,0,2:T(4,128)}, u32[]{:S(2)}) copy-start(f32[3,8,5376]{1,0,2:T(4,128)} %copy.137) | copy-start | bytes 1548292
  135.2 96.4 %copy-start.90 = (s32[1,4]{1,0:T(1,128)S(1)}, s32[1,4]{1,0:T(1,128)}, u32[]{:S(2)}) copy-start(s32[1,4]{1,0:T(1,128)} %param.23) | copy-start | bytes 52
  135.2 96.7 %copy-start.14 = (s32[4,2,8,128]{3,2,1,0:T(8,128)S(1)}, s32[4,2,8,128]{3,2,1,0:T(8,128)}, u32[]{:S(2)}) copy-start(s32[4,2,8,128]{3,2,1,0:T(8,128)} %param.24) | copy-start | bytes 98308
  227.0 6.9 collective-permute-start.1
  229.2 9.5 collective-permute-start.2
  238.7 18.1 %copy-start.6 = (f32[3,32,1,8,128]{4,1,3,2,0:T(8,128)}, f32[3,32,1,8,128]{4,1,3,2,0:T(8,128)S(1)}, u32[]{:S(2)}) copy-start(f32[3,32,1,8,128]{4,1,3,2,0:T(8,128)S(1)} %collective-permute-done.2) | copy-start | bytes 1179652
  238.8 11.1 %copy-start.15 = (f32[4,2,8,128]{3,2,1,0:T(8,128)S(1)}, f32[4,2,8,128]{3,2,1,0:T(8,128)}, u32[]{:S(2)}) copy-start(f32[4,2,8,128]{3,2,1,0:T(8,128)} %get-tuple-element.80) | copy-start | bytes 98308
  244.5 6.0 collective-permute-start.3
  247.4 5.7 collective-permute-start.4
  293.2 5.9 copy-start.78
  299.1 8.4 copy-start.81
  299.3 9.0 copy-start.3
  299.3 9.0 copy-start.4
  299.4 9.0 copy-start.7
  299.4 9.0 copy-start.79
  301.2 6.3 collective-permute-start
  308.0 5.7 copy-start.21
  308.0 5.7 copy-start.23
  308.0 5.7 copy-start.25
  308.0 5.7 copy-start.27
  308.0 5.7 copy-start.29
  308.0 5.7 copy-start.31
  308.0 5.7 copy-start.33
  308.1 5.7 copy-start.35
  308.1 5.7 copy-start.37
  308.1 5.7 copy-start.39
  308.1 5.7 copy-start.41
  308.1 5.7 copy-start.43
  308.1 5.7 copy-start.45
  308.1 5.7 copy-start.47
  308.1 5.7 copy-start.49
  308.1 5.7 copy-start.51
  308.1 5.7 copy-start.53
  308.2 5.7 copy-start.55
  308.2 5.7 copy-start.57
  308.2 5.7 copy-start.59
  663.9 8.9 collective-permute-start.5
  667.6 9.1 collective-permute-start.6
  685.4 8.2 collective-permute-start.7
  690.3 8.1 collective-permute-start.8
  716.4 348.2 %copy-start.18 = (f32[1,32,32]{1,2,0:T(8,128)S(1)}, f32[1,32,32]{1,2,0:T(8,128)}, u32[]{:S(2)}) copy-start(f32[1,32,32]{1,2,0:T(8,128)} %get-tuple-element.84) | copy-start | bytes 12292
  716.4 348.2 %copy-start.19 = (f32[1,32,32]{1,2,0:T(8,128)S(1)}, f32[1,32,32]{1,2,0:T(8,128)}, u32[]{:S(2)}) copy-start(f32[1,32,32]{1,2,0:T(8,128)} %get-tuple-element.86) | copy-start | bytes 12292
  716.4 349.0 %copy-start.20 = (f32[1,32,32]{1,2,0:T(8,128)S(1)}, f32[1,32,32]{1,2,0:T(8,128)}, u32[]{:S(2)}) copy-start(f32[1,32,32]{1,2,0:T(8,128)} %multiply_bitcast_fusion.2) | copy-start | bytes 12292
  716.4 354.5 %copy-start.1 = (f32[16]{0:T(128)S(1)}, f32[16]{0:T(128)}, u32[]{:S(2)}) copy-start(f32[16]{0:T(128)} %param.22) | copy-start | bytes 196
  (53 other events, 197.1 us)
Sparse Core Ops, SparseCore 0:
  135.3 112.6 all-gather.1
